TPU v7x, 128 devices: a whole 4x4x4 slice. The times are simulated.
128 devices in a mesh: gx: 8 (over z, core), gy: 16 (over x, y).
Axes of the slice: x: 4, y: 4, z: 4, core: 2. Of those that a mesh axis runs over, the one named last changes fastest.
Arguments:
- state_prev: float32 [256, 128, 1024], P('gy', None, 'gx'), may hold values from -60 to 60
- diffusivity: float32 [256, 128, 1024], P('gy', None, 'gx'), may hold values from 0.5 to 4
- vapour: float32 [256, 128, 1024], P('gy', None, 'gx'), may hold values from 0.01 to 0.1
- cos_zenith: float32 [256, 1024], P('gy', 'gx'), may hold values from 0.1 to 1
- albedo: float32 [256, 1024], P('gy', 'gx'), may hold values from 0.05 to 0.8
- absorption: float32 [128, 112], replicated, may hold values from 0.005 to 1
- solar_weight: float32 [112], replicated, may hold values from 0.002 to 0.02
- day_mask: int32 [2048], P(('gx', 'gy')), may hold values from 0 to 1, as said below
Outputs:
- state_next: float32 [256, 128, 1024], P('gy', None, 'gx')
- residual: float32 [256, 128, 1024], P('gy', None, 'gx')
- net_flux: float32 [256, 128, 1024], P('gy', None, 'gx')
Inputs may be any that keep to these rules, and one draw needn't show every extreme that they name: `day_mask`: exactly half of the 2048 entries are 1, and some device holds only sunlit blocks.
All inputs are finite; a program needn't handle non-finite values.
Results may differ from a plain program's by a relative error of at most 0.00015.
Values sent between devices are 32-bit elements; how exact they have to be, the bound alone decides.
No kernel may reach another device: no remote copies, remote signals or barrier semaphores. Data moves between devices by JAX's collectives and lax.ppermute only.
A program may use at most 128 MiB of HBM per device.

v0:
```python
import jax
import jax.numpy as jnp
from jax import lax
from jax.sharding import Mesh
from jax.sharding import PartitionSpec as P

ITERS = 5
GX = ("gx_0", "gx_1")
GY = ("gy_0", "gy_1")
GX_GY = ("gx_0", "gx_1", "gy_0", "gy_1")


def padded(array, sides, width, wrap):
    for axis, dim in sides:
        devices, length = (lax.axis_size(axis), array.shape[dim])
        up = [(i, (i + 1) % devices) for i in range(devices if wrap else devices - 1)]
        down = [(j, i) for i, j in up]
        last = lax.slice_in_dim(array, length - width, length, axis=dim)
        first = lax.slice_in_dim(array, 0, width, axis=dim)
        before = lax.ppermute(last, axis, up)
        after = lax.ppermute(first, axis, down)
        array = jnp.concatenate([before, array, after], axis=dim)
    return array


def one_axis_at_a_time(array, axes):
    for axis in axes:
        array = lax.psum(array, axis)
    return array


def in_order(blocks, dim):
    blocks = jnp.moveaxis(blocks, 0, dim)
    shape = blocks.shape
    return blocks.reshape(*shape[:dim], shape[dim] * shape[dim + 1], *shape[dim + 2 :])


def stacked_from(array, axes, sequence):
    blocks = array
    for k in sequence:
        blocks = lax.all_gather(blocks, axes[k])
    done = sequence[::-1]
    back = [done.index(k) for k in range(len(axes))]
    blocks = blocks.transpose(*back, *range(len(axes), blocks.ndim))
    return blocks.reshape(-1, *array.shape)


def gathered_by_axis(array, axes, sequence, dim):
    return in_order(stacked_from(array, axes, sequence), dim)


def longitude_edges(values):
    return padded(values, ((GX, 2),), 1, True)


def latitude_edges(values):
    return padded(values, ((GY, 0),), 1, False)


def face_terms(diffusivity):
    widened = longitude_edges(diffusivity)
    extended = latitude_edges(diffusivity)
    east_face = jnp.sqrt(diffusivity * widened[:, :, 2:])
    west_face = jnp.sqrt(diffusivity * widened[:, :, :-2])
    north_face = jnp.sqrt(diffusivity * extended[2:])
    south_face = jnp.sqrt(diffusivity * extended[:-2])
    level_face = jnp.sqrt(diffusivity[:, 1:] * diffusivity[:, :-1])
    return (east_face, west_face, north_face, south_face, level_face)


def operate(values, conductances):
    east_face, west_face, north_face, south_face, level_face = conductances
    widened = longitude_edges(values)
    extended = latitude_edges(values)
    applied = (
        values
        + east_face * (values - widened[:, :, 2:])
        + west_face * (values - widened[:, :, :-2])
    )
    applied = applied + north_face * (values - extended[2:]) + south_face * (values - extended[:-2])
    vertical = level_face * (values[:, 1:] - values[:, :-1])
    padding = jnp.zeros_like(values[:, :1])
    return (
        applied - jnp.concatenate([vertical, padding], 1) + jnp.concatenate([padding, vertical], 1)
    )


def squares(residual):
    return one_axis_at_a_time(jnp.sum(residual * residual), GX_GY)


def radiate(layer_amount, sunlight, triangle, absorption, solar_weight):
    levels = layer_amount.shape[0]
    columns = layer_amount.shape[1]
    gpoints = absorption.shape[1]
    thickness = absorption[:, :, None] * layer_amount[:, None, :]
    cumulative = jnp.dot(
        triangle,
        thickness.reshape(levels, gpoints * columns),
        precision=lax.Precision.HIGHEST,
        preferred_element_type=jnp.float32,
    )
    cumulative = cumulative.reshape(levels, gpoints, columns)
    cosine = sunlight[0]
    surface = sunlight[1]
    downward = cosine * jnp.exp(-cumulative / cosine)
    upward = surface * downward[-1] * jnp.exp(-1.66 * (cumulative[-1] - cumulative))
    return jnp.einsum("lgc,g->lc", downward - upward, solar_weight, precision=lax.Precision.HIGHEST)


def body(state_prev, diffusivity, vapour, cos_zenith, albedo, absorption, solar_weight, day_mask):
    conductances = face_terms(diffusivity)
    state_next = state_prev
    residual = state_prev - operate(state_prev, conductances)
    direction = residual
    current = squares(residual)
    for iteration in range(ITERS):
        applied = operate(direction, conductances)
        curvature_sum = one_axis_at_a_time(jnp.sum(direction * applied), GX_GY)
        step_size = current / curvature_sum
        state_next = state_next + step_size * direction
        residual = residual - step_size * applied
        following = squares(residual)
        direction = residual + following / current * direction
        current = following
    optical = vapour * (1.0 + 0.5 * jnp.tanh(state_prev))
    sunlight = jnp.stack([cos_zenith, albedo], 1)
    levels = optical.shape[1]
    triangle = (
        lax.broadcasted_iota(jnp.int32, (levels, levels), 0)
        >= lax.broadcasted_iota(jnp.int32, (levels, levels), 1)
    ).astype(jnp.float32)

    def slab_flux(inputs):
        return radiate(inputs[0], inputs[1], triangle, absorption, solar_weight)

    lit_blocks = day_mask.astype(jnp.float32)[:, None, None]
    whole_mask = gathered_by_axis(day_mask, GX_GY, (0, 2, 3, 1), 0)
    devices = lax.axis_size(GX) * lax.axis_size(GY)
    blocks = day_mask.shape[0]
    width = optical.shape[2]
    capacity = blocks * width // devices
    working = blocks * width // 2
    myself = lax.axis_index(GX) * lax.axis_size(GY) + lax.axis_index(GY)
    per_device = jnp.sum(whole_mask.reshape(devices, blocks), 1)
    ends = jnp.cumsum(per_device) * width
    starts = ends - per_device * width
    my_start = jnp.take(starts, myself)
    my_end = jnp.take(ends, myself)
    own_rank = jnp.cumsum(day_mask) - 1
    peer_ids = lax.broadcasted_iota(jnp.int32, (devices, capacity), 0)
    slot_ids = lax.broadcasted_iota(jnp.int32, (devices, capacity), 1)
    first = my_start + (peer_ids - my_start) % devices
    wanted = first + slot_ids * devices
    valid_send = (wanted < my_end).astype(jnp.float32)
    offset = wanted - my_start
    rank_needed = offset // width
    row_hits = (own_rank[None, None, :] == rank_needed[:, :, None]) & (day_mask[None, None, :] == 1)
    row_ids = lax.broadcasted_iota(jnp.int32, (1, 1, blocks), 2)
    row_of = jnp.sum(jnp.where(row_hits, row_ids, 0), 2)
    flat_send = jnp.clip(row_of * width + offset % width, 0, blocks * width - 1)
    packed = jnp.concatenate([optical, sunlight], 1)
    packed = jnp.transpose(packed, (1, 0, 2)).reshape(levels + 2, blocks * width)
    outgoing = jnp.take(packed, flat_send.reshape(-1), 1).reshape(levels + 2, devices, capacity)
    outgoing = jnp.transpose(outgoing * valid_send[None], (1, 0, 2))
    arrived = lax.all_to_all(outgoing, GX_GY, split_axis=0, concat_axis=0, tiled=True)
    work_ids = lax.broadcasted_iota(jnp.int32, (working,), 0)
    global_ids = work_ids * devices + myself
    source = jnp.sum((ends[None, :] <= global_ids[:, None]).astype(jnp.int32), 1)
    source = jnp.clip(source, 0, devices - 1)
    source_start = jnp.take(starts, source)
    source_first = source_start + (myself - source_start) % devices
    flat_work = jnp.clip(
        source * capacity + (global_ids - source_first) // devices, 0, devices * capacity - 1
    )
    arrived_flat = jnp.transpose(arrived, (1, 0, 2)).reshape(levels + 2, devices * capacity)
    work = jnp.take(arrived_flat, flat_work, 1).reshape(levels + 2, working // width, width)
    work = jnp.transpose(work, (1, 0, 2))
    fluxes = lax.map(slab_flux, (work[:, :levels], work[:, levels:]))
    fluxes = jnp.transpose(fluxes, (1, 0, 2)).reshape(levels, working)
    peer_start = starts[:, None]
    back_ids = peer_start + (myself - peer_start) % devices + slot_ids * devices
    valid_back = (back_ids < ends[:, None]).astype(jnp.float32)
    back_slot = jnp.clip((back_ids - myself) // devices, 0, working - 1)
    returning = jnp.take(fluxes, back_slot.reshape(-1), 1).reshape(levels, devices, capacity)
    returning = jnp.transpose(returning * valid_back[None], (1, 0, 2))
    came_back = lax.all_to_all(returning, GX_GY, split_axis=0, concat_axis=0, tiled=True)
    column_ids = lax.broadcasted_iota(jnp.int32, (blocks, width), 1)
    own_ids = my_start + jnp.clip(own_rank, 0, blocks - 1)[:, None] * width + column_ids
    home_peer = own_ids % devices
    home_first = my_start + (home_peer - my_start) % devices
    flat_home = jnp.clip(
        home_peer * capacity + (own_ids - home_first) // devices, 0, devices * capacity - 1
    )
    back_flat = jnp.transpose(came_back, (1, 0, 2)).reshape(levels, devices * capacity)
    placed = jnp.take(back_flat, flat_home.reshape(-1), 1).reshape(levels, blocks, width)
    net_flux = jnp.transpose(placed, (1, 0, 2)) * lit_blocks
    return (state_next, residual, net_flux)


def solution(mesh):
    torus = Mesh(mesh.devices.reshape(4, 2, 4, 4), ("gx_0", "gx_1", "gy_0", "gy_1"))
    in_specs = (
        P(GY, None, GX),
        P(GY, None, GX),
        P(GY, None, GX),
        P(GY, GX),
        P(GY, GX),
        P(),
        P(),
        P(GX_GY),
    )
    out_specs = (P(GY, None, GX), P(GY, None, GX), P(GY, None, GX))
    return jax.shard_map(body, mesh=torus, in_specs=in_specs, out_specs=out_specs, check_vma=False)
```

profile of v0, /device:TPU:0, one launch (start us, length us, event | category | flops | bytes accessed | tf_op | source)
XLA Modules:
  0.0 903.1 jit_solution(10297394391904766983)
XLA Ops:
  20.8 7.3 all-reduce.12
  28.2 14.2 %all-gather.4 = s32[4,4,16]{2,1,0:T(4,128)S(1)} all-gather(s32[1,4,16]{2,1,0:T(4,128)S(1)} %reshape.966), channel_id=3, replica_groups=mesh['gx_0'=4,'gx_1'=2,'gy_0'=4,'gy_1'=4] {'gy_0'}, dimensions={0}, use_global_device_ids=true | all-gather | bytes 1280 | tf_op jit(solution)/shard_map/all_gather | solution.py:41
  42.5 11.9 %all-gather.2 = s32[16,4,16]{2,1,0:T(4,128)S(1)} all-gather(s32[4,4,16]{2,1,0:T(4,128)S(1)} %all-gather.4), channel_id=4, replica_groups=mesh['gx_0'=4,'gx_1'=2,'gy_0'=4,'gy_1'=4] {'gy_1'}, dimensions={0}, use_global_device_ids=true | all-gather | bytes 5120 | tf_op jit(solution)/shard_map/all_gather | solution.py:41
  76.0 6.5 fusion.100
  97.6 9.4 %all-reduce.15 = (f32[]{:T(128)}, f32[]{:T(128)}) all-reduce(f32[]{:T(128)} %get-tuple-element.87, f32[]{:T(128)} %get-tuple-element.86), channel_id=1, replica_groups=mesh['gx_0'=4,'gx_1'=2,'gy_0'=4,'gy_1'=4] {'gx_0'}, use_global_device_ids=true, to_apply=%region_1.0 | all-reduce | flops 2 | bytes 16 | tf_op jit(solution)/shard_map/psum | solution.py:28
  110.2 15.7 %all-reduce.14 = (f32[]{:T(128)}, f32[]{:T(128)}) all-reduce(f32[]{:T(128)} %get-tuple-element.106, f32[]{:T(128)} %get-tuple-element.107), channel_id=1, replica_groups=mesh['gx_0'=4,'gx_1'=2,'gy_0'=4,'gy_1'=4] {'gy_0'}, use_global_device_ids=true, to_apply=%region_3.0 | all-reduce | flops 2 | bytes 16 | tf_op jit(solution)/shard_map/psum | solution.py:28
  125.9 10.1 %all-reduce.13 = (f32[]{:T(128)}, f32[]{:T(128)}) all-reduce(f32[]{:T(128)} %get-tuple-element.102, f32[]{:T(128)} %get-tuple-element.103), channel_id=1, replica_groups=mesh['gx_0'=4,'gx_1'=2,'gy_0'=4,'gy_1'=4] {'gy_1'}, use_global_device_ids=true, to_apply=%region_4.0 | all-reduce | flops 2 | bytes 16 | tf_op jit(solution)/shard_map/psum | solution.py:28
  139.5 9.3 %psum.288 = f32[]{:T(128)} all-reduce(f32[]{:T(128)} %multiply_reduce_fusion.7), channel_id=1, replica_groups=mesh['gx_0'=4,'gx_1'=2,'gy_0'=4,'gy_1'=4] {'gx_0'}, use_global_device_ids=true, to_apply=%region_11.0 | all-reduce | flops 1 | bytes 8 | tf_op jit(solution)/shard_map/psum | solution.py:28
  153.3 8.5 psum.290
  163.7 9.1 %psum.291 = f32[]{:T(128)} all-reduce(f32[]{:T(128)} %psum.290), channel_id=1, replica_groups=mesh['gx_0'=4,'gx_1'=2,'gy_0'=4,'gy_1'=4] {'gy_1'}, use_global_device_ids=true, to_apply=%region_14.0 | all-reduce | flops 1 | bytes 8 | tf_op jit(solution)/shard_map/psum | solution.py:28
  189.4 9.4 %psum.292 = f32[]{:T(128)} all-reduce(f32[]{:T(128)} %get-tuple-element.122), channel_id=1, replica_groups=mesh['gx_0'=4,'gx_1'=2,'gy_0'=4,'gy_1'=4] {'gx_0'}, use_global_device_ids=true, to_apply=%region_16.0 | all-reduce | flops 1 | bytes 8 | tf_op jit(solution)/shard_map/psum | solution.py:28
  202.1 12.7 %psum.294 = f32[]{:T(128)} all-reduce(f32[]{:T(128)} %psum.293), channel_id=1, replica_groups=mesh['gx_0'=4,'gx_1'=2,'gy_0'=4,'gy_1'=4] {'gy_0'}, use_global_device_ids=true, to_apply=%region_18.0 | all-reduce | flops 1 | bytes 8 | tf_op jit(solution)/shard_map/psum | solution.py:28
  214.8 10.1 %gather_fusion.1 = f32[2048,130]{1,0:T(8,128)} fusion(f32[130,2048]{0,1:T(8,128)} %bitcast.117, s32[2048]{0:T(1024)S(1)} %broadcast_clamp_fusion.2), kind=kCustom, calls=%fused_computation.1 | custom fusion | bytes 2138112 | tf_op jit(solution)/shard_map/jit(_take)/gather | solution.py:164
  224.9 8.7 psum.295
  238.5 9.5 %psum.296 = f32[]{:T(128)} all-reduce(f32[]{:T(128)} %get-tuple-element.120), channel_id=1, replica_groups=mesh['gx_0'=4,'gx_1'=2,'gy_0'=4,'gy_1'=4] {'gx_0'}, use_global_device_ids=true, to_apply=%region_21.0 | all-reduce | flops 1 | bytes 8 | tf_op jit(solution)/shard_map/psum | solution.py:28
  259.9 27.5 %psum.298 = f32[]{:T(128)} all-reduce(f32[]{:T(128)} %psum.297), channel_id=1, replica_groups=mesh['gx_0'=4,'gx_1'=2,'gy_0'=4,'gy_1'=4] {'gy_0'}, use_global_device_ids=true, to_apply=%region_23.0 | all-reduce | flops 1 | bytes 8 | tf_op jit(solution)/shard_map/psum | solution.py:28
  288.0 11.3 %psum.299 = f32[]{:T(128)} all-reduce(f32[]{:T(128)} %psum.298), channel_id=1, replica_groups=mesh['gx_0'=4,'gx_1'=2,'gy_0'=4,'gy_1'=4] {'gy_1'}, use_global_device_ids=true, to_apply=%region_24.0 | all-reduce | flops 1 | bytes 8 | tf_op jit(solution)/shard_map/psum | solution.py:28
  313.5 11.8 %psum.300 = f32[]{:T(128)} all-reduce(f32[]{:T(128)} %get-tuple-element.118), channel_id=1, replica_groups=mesh['gx_0'=4,'gx_1'=2,'gy_0'=4,'gy_1'=4] {'gx_0'}, use_global_device_ids=true, to_apply=%region_26.0 | all-reduce | flops 1 | bytes 8 | tf_op jit(solution)/shard_map/psum | solution.py:28
  328.7 13.1 %psum.302 = f32[]{:T(128)} all-reduce(f32[]{:T(128)} %psum.301), channel_id=1, replica_groups=mesh['gx_0'=4,'gx_1'=2,'gy_0'=4,'gy_1'=4] {'gy_0'}, use_global_device_ids=true, to_apply=%region_28.0 | all-reduce | flops 1 | bytes 8 | tf_op jit(solution)/shard_map/psum | solution.py:28
  341.8 9.5 %psum.303 = f32[]{:T(128)} all-reduce(f32[]{:T(128)} %psum.302), channel_id=1, replica_groups=mesh['gx_0'=4,'gx_1'=2,'gy_0'=4,'gy_1'=4] {'gy_1'}, use_global_device_ids=true, to_apply=%region_29.0 | all-reduce | flops 1 | bytes 8 | tf_op jit(solution)/shard_map/psum | solution.py:28
  355.7 8.3 psum.304
  367.0 10.2 %psum.306 = f32[]{:T(128)} all-reduce(f32[]{:T(128)} %psum.305), channel_id=1, replica_groups=mesh['gx_0'=4,'gx_1'=2,'gy_0'=4,'gy_1'=4] {'gy_0'}, use_global_device_ids=true, to_apply=%region_33.0 | all-reduce | flops 1 | bytes 8 | tf_op jit(solution)/shard_map/psum | solution.py:28
  377.2 6.6 gather_fusion
  383.7 8.2 psum.307
  409.3 10.4 %psum.308 = f32[]{:T(128)} all-reduce(f32[]{:T(128)} %get-tuple-element.114), channel_id=1, replica_groups=mesh['gx_0'=4,'gx_1'=2,'gy_0'=4,'gy_1'=4] {'gx_0'}, use_global_device_ids=true, to_apply=%region_36.0 | all-reduce | flops 1 | bytes 8 | tf_op jit(solution)/shard_map/psum | solution.py:28
  422.9 10.3 %psum.310 = f32[]{:T(128)} all-reduce(f32[]{:T(128)} %psum.309), channel_id=1, replica_groups=mesh['gx_0'=4,'gx_1'=2,'gy_0'=4,'gy_1'=4] {'gy_0'}, use_global_device_ids=true, to_apply=%region_38.0 | all-reduce | flops 1 | bytes 8 | tf_op jit(solution)/shard_map/psum | solution.py:28
  433.2 9.9 %psum.311 = f32[]{:T(128)} all-reduce(f32[]{:T(128)} %psum.310), channel_id=1, replica_groups=mesh['gx_0'=4,'gx_1'=2,'gy_0'=4,'gy_1'=4] {'gy_1'}, use_global_device_ids=true, to_apply=%region_39.0 | all-reduce | flops 1 | bytes 8 | tf_op jit(solution)/shard_map/psum | solution.py:28
  447.7 8.4 psum.312
  459.9 10.2 %psum.314 = f32[]{:T(128)} all-reduce(f32[]{:T(128)} %psum.313), channel_id=1, replica_groups=mesh['gx_0'=4,'gx_1'=2,'gy_0'=4,'gy_1'=4] {'gy_0'}, use_global_device_ids=true, to_apply=%region_43.0 | all-reduce | flops 1 | bytes 8 | tf_op jit(solution)/shard_map/psum | solution.py:28
  470.8 8.4 psum.315
  498.7 325.5 %while.13 = (s32[]{:T(128)}, f32[8,128,128]{2,1,0:T(8,128)}, f32[8,2,128]{2,1,0:T(2,128)S(1)}, f32[128,112]{0,1:T(8,128)S(1)}, f32[8,128,128]{2,1,0:T(8,128)S(1)}, /*index=5*/f32[112]{0:T(128)S(1)}, s32[]{:T(128)}) while((s32[]{:T(128)}, f32[8,128,128]{2,1,0:T(8,128)}, f32[8,2,128]{2,1,0:T(2,128)S(1)}, ...), condition=%wide.region_56.57_spmd.clone, body=%wide.region_55.56_spmd.clone.sunk | while | flops 2860824576 | bytes 88995904 | solution.py:179
  501.3 15.5 %fusion.207 = f32[14336,128]{1,0:T(8,128)} fusion(f32[16,8,112,128]{3,2,1,0:T(8,128)S(1)} %bitcast.114), kind=kOutput, calls=%fused_computation.6.clone.1 | convolution fusion | flops 2818605056 | bytes 14680064 | tf_op jit(solution)/shard_map/while/body/eval_jaxpr/dot_general | solution.py:97
  516.8 8.5 copy.207
  525.3 6.2 slice_reduce_fusion.2
  532.7 6.4 fusion.209
  541.9 15.5 %fusion.207 = f32[14336,128]{1,0:T(8,128)} fusion(f32[16,8,112,128]{3,2,1,0:T(8,128)S(1)} %bitcast.114), kind=kOutput, calls=%fused_computation.6.clone.1 | convolution fusion | flops 2818605056 | bytes 14680064 | tf_op jit(solution)/shard_map/while/body/eval_jaxpr/dot_general | solution.py:97
  557.4 8.5 copy.207
  573.3 6.4 fusion.209
  582.6 15.5 %fusion.207 = f32[14336,128]{1,0:T(8,128)} fusion(f32[16,8,112,128]{3,2,1,0:T(8,128)S(1)} %bitcast.114), kind=kOutput, calls=%fused_computation.6.clone.1 | convolution fusion | flops 2818605056 | bytes 14680064 | tf_op jit(solution)/shard_map/while/body/eval_jaxpr/dot_general | solution.py:97
  598.1 8.5 copy.207
  606.5 6.2 slice_reduce_fusion.2
  613.9 6.4 fusion.209
  623.2 15.5 %fusion.207 = f32[14336,128]{1,0:T(8,128)} fusion(f32[16,8,112,128]{3,2,1,0:T(8,128)S(1)} %bitcast.114), kind=kOutput, calls=%fused_computation.6.clone.1 | convolution fusion | flops 2818605056 | bytes 14680064 | tf_op jit(solution)/shard_map/while/body/eval_jaxpr/dot_general | solution.py:97
  638.7 8.5 copy.207
  654.6 6.4 fusion.209
  663.8 15.5 %fusion.207 = f32[14336,128]{1,0:T(8,128)} fusion(f32[16,8,112,128]{3,2,1,0:T(8,128)S(1)} %bitcast.114), kind=kOutput, calls=%fused_computation.6.clone.1 | convolution fusion | flops 2818605056 | bytes 14680064 | tf_op jit(solution)/shard_map/while/body/eval_jaxpr/dot_general | solution.py:97
  679.3 8.5 copy.207
  687.7 6.2 slice_reduce_fusion.2
  695.2 6.4 fusion.209
  704.4 15.5 %fusion.207 = f32[14336,128]{1,0:T(8,128)} fusion(f32[16,8,112,128]{3,2,1,0:T(8,128)S(1)} %bitcast.114), kind=kOutput, calls=%fused_computation.6.clone.1 | convolution fusion | flops 2818605056 | bytes 14680064 | tf_op jit(solution)/shard_map/while/body/eval_jaxpr/dot_general | solution.py:97
  719.9 8.5 copy.207
  735.8 6.4 fusion.209
  745.0 15.5 %fusion.207 = f32[14336,128]{1,0:T(8,128)} fusion(f32[16,8,112,128]{3,2,1,0:T(8,128)S(1)} %bitcast.114), kind=kOutput, calls=%fused_computation.6.clone.1 | convolution fusion | flops 2818605056 | bytes 14680064 | tf_op jit(solution)/shard_map/while/body/eval_jaxpr/dot_general | solution.py:97
  760.5 8.5 copy.207
  776.4 6.4 fusion.209
  785.6 15.5 %fusion.207 = f32[14336,128]{1,0:T(8,128)} fusion(f32[16,8,112,128]{3,2,1,0:T(8,128)S(1)} %bitcast.114), kind=kOutput, calls=%fused_computation.6.clone.1 | convolution fusion | flops 2818605056 | bytes 14680064 | tf_op jit(solution)/shard_map/while/body/eval_jaxpr/dot_general | solution.py:97
  801.1 8.5 copy.207
  809.6 6.2 slice_reduce_fusion.2
  817.0 6.4 fusion.209
  825.7 7.6 gather_fusion.3
  841.7 7.7 multiply_reduce_fusion
  849.4 11.2 %psum.316 = f32[]{:T(128)} all-reduce(f32[]{:T(128)} %get-tuple-element.110), channel_id=1, replica_groups=mesh['gx_0'=4,'gx_1'=2,'gy_0'=4,'gy_1'=4] {'gx_0'}, use_global_device_ids=true, to_apply=%region_46.0 | all-reduce | flops 1 | bytes 8 | tf_op jit(solution)/shard_map/psum | solution.py:28
  863.8 11.1 %psum.318 = f32[]{:T(128)} all-reduce(f32[]{:T(128)} %psum.317), channel_id=1, replica_groups=mesh['gx_0'=4,'gx_1'=2,'gy_0'=4,'gy_1'=4] {'gy_0'}, use_global_device_ids=true, to_apply=%region_48.0 | all-reduce | flops 1 | bytes 8 | tf_op jit(solution)/shard_map/psum | solution.py:28
  874.9 11.2 %psum.319 = f32[]{:T(128)} all-reduce(f32[]{:T(128)} %psum.318), channel_id=1, replica_groups=mesh['gx_0'=4,'gx_1'=2,'gy_0'=4,'gy_1'=4] {'gy_1'}, use_global_device_ids=true, to_apply=%region_49.0 | all-reduce | flops 1 | bytes 8 | tf_op jit(solution)/shard_map/psum | solution.py:28
  (355 shorter events, 253.3 us)
Async XLA Ops:
  0.6 18.7 %copy-start.44 = (u32[128]{0:T(128)S(1)}, u32[128]{0:T(128)}, u32[]{:S(2)}) copy-start(u32[128]{0:T(128)} %constant.319) | copy-start | bytes 1540
  0.6 19.9 %copy-start.41 = (s32[16]{0:T(128)S(1)}, s32[16]{0:T(128)}, u32[]{:S(2)}) copy-start(s32[16]{0:T(128)} %param.17) | copy-start | bytes 196
  2.3 73.2 %collective-permute-start.7 = (f32[1,128,128]{1,0,2:T(1,128)}, f32[1,128,128]{1,0,2:T(1,128)S(1)}, u32[]{:S(2)}, u32[]{:S(2)}) collective-permute-start(f32[1,128,128]{1,0,2:T(1,128)} %copy.162), channel_id=1, source_target_pairs={{0,1},{1,2},{2,3},{3,4},{4,5},{5,6},{6,7},{7,8},{8,9},{9,10},{10,1... | collective-permute-start | bytes 196616 | tf_op jit(solution)/shard_map/ppermute | solution.py:20
  6.5 68.9 %collective-permute-start.5 = (f32[1,128,128]{1,0,2:T(1,128)}, f32[1,128,128]{1,0,2:T(1,128)}, u32[]{:S(2)}, u32[]{:S(2)}) collective-permute-start(f32[1,128,128]{1,0,2:T(1,128)} %copy.156), channel_id=1, source_target_pairs={{1,0},{2,1},{3,2},{4,3},{5,4},{6,5},{7,6},{8,7},{9,8},{10,9},{11,1... | collective-permute-start | bytes 196616 | tf_op jit(solution)/shard_map/ppermute | solution.py:21
  9.6 48.5 %copy-start.11 = (f32[16,128,128]{1,0,2:T(8,128)}, f32[16,128,128]{1,0,2:T(8,128)S(1)}, u32[]{:S(2)}) copy-start(f32[16,128,128]{1,0,2:T(8,128)S(1)} %copy.170) | copy-start | bytes 3145732
  10.2 57.5 %collective-permute-start.3 = (f32[16,128,1]{1,0,2:T(8,128)}, f32[16,128,1]{1,0,2:T(8,128)S(1)}, u32[]{:S(2)}, u32[]{:S(2)}) collective-permute-start(f32[16,128,1]{1,0,2:T(8,128)} %get-tuple-element.154), channel_id=1, source_target_pairs={{0,16},{16,32},{32,48},{48,64},{64,80},{80,96},{96,112},{112,0},{1... | collective-permute-start | bytes 24584 | tf_op jit(solution)/shard_map/ppermute | solution.py:20
  10.2 57.6 %collective-permute-start.1 = (f32[16,128,1]{1,0,2:T(8,128)S(1)}, f32[16,128,1]{1,0,2:T(8,128)S(1)}, u32[]{:S(2)}, u32[]{:S(2)}) collective-permute-start(f32[16,128,1]{1,0,2:T(8,128)S(1)} %get-tuple-element.153), channel_id=1, source_target_pairs={{16,0},{32,16},{48,32},{64,48},{80,64},{96,80},{112,96},{0,112},{1... | collective-permute-start | bytes 24584 | tf_op jit(solution)/shard_map/ppermute | solution.py:21
  15.2 389.7 %copy-start.1 = (f32[16,128,128]{1,0,2:T(8,128)}, f32[16,128,128]{1,0,2:T(8,128)S(1)}, u32[]{:S(2)}) copy-start(f32[16,128,128]{1,0,2:T(8,128)S(1)} %copy.142) | copy-start | bytes 3145732
  15.2 54.0 %collective-permute-start = (f32[16,128,1]{1,0,2:T(8,128)S(1)}, f32[16,128,1]{1,0,2:T(8,128)S(1)}, u32[]{:S(2)}, u32[]{:S(2)}) collective-permute-start(f32[16,128,1]{1,0,2:T(8,128)S(1)} %get-tuple-element.152), channel_id=1, source_target_pairs={{16,0},{32,16},{48,32},{64,48},{80,64},{96,80},{112,96},{0,112},{1... | collective-permute-start | bytes 24584 | tf_op jit(solution)/shard_map/ppermute | solution.py:21
  17.7 79.9 %copy-start.8 = (f32[16,127,128]{1,0,2:T(8,128)}, f32[16,127,128]{1,0,2:T(8,128)S(1)}, u32[]{:S(2)}) copy-start(f32[16,127,128]{1,0,2:T(8,128)S(1)} %get-tuple-element.126) | copy-start | bytes 3121156
  67.7 7.8 collective-permute-start.2
  67.9 7.6 collective-permute-start.4
  69.2 335.7 %copy-start.17 = (f32[16,128,1]{1,0,2:T(8,128)}, f32[16,128,1]{1,0,2:T(8,128)S(1)}, u32[]{:S(2)}) copy-start(f32[16,128,1]{1,0,2:T(8,128)S(1)} %collective-permute-done) | copy-start | bytes 24580
  69.2 6.8 collective-permute-start.6
  75.5 329.4 %copy-start.19 = (f32[16,128,1]{1,0,2:T(8,128)}, f32[16,128,1]{1,0,2:T(8,128)S(1)}, u32[]{:S(2)}) copy-start(f32[16,128,1]{1,0,2:T(8,128)S(1)} %collective-permute-done.2) | copy-start | bytes 24580
  75.5 329.4 %copy-start.12 = (f32[1,128,128]{1,0,2:T(1,128)}, f32[1,128,128]{1,0,2:T(1,128)S(1)}, u32[]{:S(2)}) copy-start(f32[1,128,128]{1,0,2:T(1,128)S(1)} %collective-permute-done.4) | copy-start | bytes 196612
  75.9 329.0 %copy-start.14 = (f32[1,128,128]{1,0,2:T(1,128)}, f32[1,128,128]{1,0,2:T(1,128)S(1)}, u32[]{:S(2)}) copy-start(f32[1,128,128]{1,0,2:T(1,128)S(1)} %collective-permute-done.6) | copy-start | bytes 196612
  75.9 63.4 %copy-start.28 = (s32[128]{0:T(128)S(1)}, s32[128]{0:T(128)}, u32[]{:S(2)}) copy-start(s32[128]{0:T(128)} %copy-done.27) | copy-start | bytes 1540
  75.9 63.4 %copy-start.29 = (s32[16]{0:T(128)S(1)}, s32[16]{0:T(128)}, u32[]{:S(2)}) copy-start(s32[16]{0:T(128)} %iota_multiply_fusion) | copy-start | bytes 196
  75.9 63.4 %copy-start.31 = (s32[128]{0:T(128)S(1)}, s32[128]{0:T(128)}, u32[]{:S(2)}) copy-start(s32[128]{0:T(128)} %copy-done.30) | copy-start | bytes 1540
  75.9 63.4 %copy-start.33 = (s32[128]{0:T(128)S(1)}, s32[128]{0:T(128)}, u32[]{:S(2)}) copy-start(s32[128]{0:T(128)} %copy-done.32) | copy-start | bytes 1540
  75.9 63.4 %copy-start.35 = (s32[128]{0:T(128)S(1)}, s32[128]{0:T(128)}, u32[]{:S(2)}) copy-start(s32[128]{0:T(128)} %copy-done.34) | copy-start | bytes 1540
  75.9 63.4 %copy-start.37 = (pred[128]{0:T(512)(128)(4,1)S(1)}, pred[128]{0:T(512)(128)(4,1)}, u32[]{:S(2)}) copy-start(pred[128]{0:T(512)(128)(4,1)} %copy-done.36) | copy-start | bytes 388
  76.0 63.4 %copy-start.40 = (s32[128]{0:T(128)S(1)}, s32[128]{0:T(128)}, u32[]{:S(2)}) copy-start(s32[128]{0:T(128)} %fusion.174) | copy-start | bytes 1540
  76.0 76.0 %copy-start.25 = (f32[16,128]{1,0:T(8,128)S(1)}, f32[16,128]{1,0:T(8,128)}, u32[]{:S(2)}) copy-start(f32[16,128]{1,0:T(8,128)} %param.14) | copy-start | bytes 24580
  76.0 76.0 %copy-start.26 = (f32[16,128]{1,0:T(8,128)S(1)}, f32[16,128]{1,0:T(8,128)}, u32[]{:S(2)}) copy-start(f32[16,128]{1,0:T(8,128)} %param.13) | copy-start | bytes 24580
  82.4 152.6 %copy-start.3 = (f32[16,128,128]{1,0,2:T(8,128)}, f32[16,128,128]{1,0,2:T(8,128)S(1)}, u32[]{:S(2)}) copy-start(f32[16,128,128]{1,0,2:T(8,128)S(1)} %fusion.100) | copy-start | bytes 3145732
  82.6 10.0 %collective-permute-start.11 = (f32[1,128,128]{1,0,2:T(1,128)S(1)}, f32[1,128,128]{1,0,2:T(1,128)S(1)}, u32[]{:S(2)}, u32[]{:S(2)}) collective-permute-start(f32[1,128,128]{1,0,2:T(1,128)S(1)} %get-tuple-element.148), channel_id=1, source_target_pairs={{0,1},{1,2},{2,3},{3,4},{4,5},{5,6},{6,7},{7,8},{8,9},{9,10},{10,1... | collective-permute-start | bytes 196616 | tf_op jit(solution)/shard_map/ppermute | solution.py:20
  87.0 6.2 collective-permute-start.10
  88.3 4.3 collective-permute-start.9
  88.3 4.3 collective-permute-start.8
  175.4 125.3 %copy-start.5 = (f32[16,128,128]{1,0,2:T(8,128)}, f32[16,128,128]{1,0,2:T(8,128)S(1)}, u32[]{:S(2)}) copy-start(f32[16,128,128]{1,0,2:T(8,128)S(1)} %multiply_add_fusion.4) | copy-start | bytes 3145732
  175.5 9.3 %collective-permute-start.15 = (f32[1,128,128]{1,0,2:T(1,128)S(1)}, f32[1,128,128]{1,0,2:T(1,128)S(1)}, u32[]{:S(2)}, u32[]{:S(2)}) collective-permute-start(f32[1,128,128]{1,0,2:T(1,128)S(1)} %get-tuple-element.144), channel_id=1, source_target_pairs={{0,1},{1,2},{2,3},{3,4},{4,5},{5,6},{6,7},{7,8},{8,9},{9,10},{10,1... | collective-permute-start | bytes 196616 | tf_op jit(solution)/shard_map/ppermute | solution.py:20
  178.8 6.2 collective-permute-start.14
  180.3 4.5 collective-permute-start.13
  180.3 4.5 collective-permute-start.12
  254.1 239.0 %all-to-all-start = ((f32[128,130,16]{1,2,0:T(8,128)}), f32[128,130,16]{1,2,0:T(8,128)}, u32[]{:S(2)}, u32[]{:S(2)}) async-start(f32[128,130,16]{1,2,0:T(8,128)} %multiply_bitcast_fusion), calls=%async_computation | async-start | bytes 4194304 | tf_op jit(solution)/shard_map/all_to_all | solution.py:166
  302.1 91.2 %copy-start.6 = (f32[16,128,128]{1,0,2:T(8,128)}, f32[16,128,128]{1,0,2:T(8,128)S(1)}, u32[]{:S(2)}) copy-start(f32[16,128,128]{1,0,2:T(8,128)S(1)} %multiply_add_fusion.3) | copy-start | bytes 3145732
  302.2 7.4 collective-permute-start.19
  303.7 6.2 collective-permute-start.18
  305.0 4.5 collective-permute-start.17
  305.1 4.5 collective-permute-start.16
  394.7 87.0 %copy-start.7 = (f32[16,128,128]{1,0,2:T(8,128)}, f32[16,128,128]{1,0,2:T(8,128)S(1)}, u32[]{:S(2)}) copy-start(f32[16,128,128]{1,0,2:T(8,128)S(1)} %multiply_add_fusion.2) | copy-start | bytes 3145732
  394.8 9.8 %collective-permute-start.23 = (f32[1,128,128]{1,0,2:T(1,128)S(1)}, f32[1,128,128]{1,0,2:T(1,128)S(1)}, u32[]{:S(2)}, u32[]{:S(2)}) collective-permute-start(f32[1,128,128]{1,0,2:T(1,128)S(1)} %get-tuple-element.136), channel_id=1, source_target_pairs={{0,1},{1,2},{2,3},{3,4},{4,5},{5,6},{6,7},{7,8},{8,9},{9,10},{10,1... | collective-permute-start | bytes 196616 | tf_op jit(solution)/shard_map/ppermute | solution.py:20
  398.7 6.2 collective-permute-start.22
  400.0 4.5 collective-permute-start.21
  400.0 91.8 %copy-start.9 = (f32[16,127,128]{1,0,2:T(8,128)S(1)}, f32[16,127,128]{1,0,2:T(8,128)}, u32[]{:S(2)}) copy-start(f32[16,127,128]{1,0,2:T(8,128)} %copy-done.8) | copy-start | bytes 3121156
  400.0 4.5 collective-permute-start.20
  481.7 17.0 %copy-start.10 = (f32[16,128,128]{1,0,2:T(8,128)}, f32[16,128,128]{1,0,2:T(8,128)S(1)}, u32[]{:S(2)}) copy-start(f32[16,128,128]{1,0,2:T(8,128)S(1)} %multiply_add_fusion.1) | copy-start | bytes 3145732
  482.5 359.1 %collective-permute-start.27 = (f32[1,128,128]{1,0,2:T(1,128)}, f32[1,128,128]{1,0,2:T(1,128)}, u32[]{:S(2)}, u32[]{:S(2)}) collective-permute-start(f32[1,128,128]{1,0,2:T(1,128)} %get-tuple-element.132), channel_id=1, source_target_pairs={{0,1},{1,2},{2,3},{3,4},{4,5},{5,6},{6,7},{7,8},{8,9},{9,10},{10,1... | collective-permute-start | bytes 196616 | tf_op jit(solution)/shard_map/ppermute | solution.py:20
  487.0 354.6 %collective-permute-start.26 = (f32[1,128,128]{1,0,2:T(1,128)}, f32[1,128,128]{1,0,2:T(1,128)}, u32[]{:S(2)}, u32[]{:S(2)}) collective-permute-start(f32[1,128,128]{1,0,2:T(1,128)} %get-tuple-element.131), channel_id=1, source_target_pairs={{1,0},{2,1},{3,2},{4,3},{5,4},{6,5},{7,6},{8,7},{9,8},{10,9},{11,1... | collective-permute-start | bytes 196616 | tf_op jit(solution)/shard_map/ppermute | solution.py:21
  488.9 352.7 %collective-permute-start.25 = (f32[16,128,1]{1,0,2:T(8,128)}, f32[16,128,1]{1,0,2:T(8,128)}, u32[]{:S(2)}, u32[]{:S(2)}) collective-permute-start(f32[16,128,1]{1,0,2:T(8,128)} %get-tuple-element.130), channel_id=1, source_target_pairs={{0,16},{16,32},{32,48},{48,64},{64,80},{80,96},{96,112},{112,0},{1... | collective-permute-start | bytes 24584 | tf_op jit(solution)/shard_map/ppermute | solution.py:20
  488.9 352.7 %collective-permute-start.24 = (f32[16,128,1]{1,0,2:T(8,128)}, f32[16,128,1]{1,0,2:T(8,128)}, u32[]{:S(2)}, u32[]{:S(2)}) collective-permute-start(f32[16,128,1]{1,0,2:T(8,128)} %get-tuple-element.129), channel_id=1, source_target_pairs={{16,0},{32,16},{48,32},{64,48},{80,64},{96,80},{112,96},{0,112},{1... | collective-permute-start | bytes 24584 | tf_op jit(solution)/shard_map/ppermute | solution.py:21
  498.7 326.9 %copy-start.24 = (s32[2048]{0:T(1024)S(1)}, s32[2048]{0:T(1024)}, u32[]{:S(2)}) copy-start(s32[2048]{0:T(1024)} %broadcast_clamp_fusion) | copy-start | bytes 24580
  824.2 17.4 %copy-start.2 = (f32[16,128,128]{1,0,2:T(8,128)S(1)}, f32[16,128,128]{1,0,2:T(8,128)}, u32[]{:S(2)}) copy-start(f32[16,128,128]{1,0,2:T(8,128)} %copy-done.1) | copy-start | bytes 3145732
  824.2 17.4 %copy-start.13 = (f32[1,128,128]{1,0,2:T(1,128)S(1)}, f32[1,128,128]{1,0,2:T(1,128)}, u32[]{:S(2)}) copy-start(f32[1,128,128]{1,0,2:T(1,128)} %copy-done.12) | copy-start | bytes 196612
  824.3 17.4 %copy-start.15 = (f32[1,128,128]{1,0,2:T(1,128)S(1)}, f32[1,128,128]{1,0,2:T(1,128)}, u32[]{:S(2)}) copy-start(f32[1,128,128]{1,0,2:T(1,128)} %copy-done.14) | copy-start | bytes 196612
  824.3 17.4 %copy-start.18 = (f32[16,128,1]{1,0,2:T(8,128)S(1)}, f32[16,128,1]{1,0,2:T(8,128)}, u32[]{:S(2)}) copy-start(f32[16,128,1]{1,0,2:T(8,128)} %copy-done.17) | copy-start | bytes 24580
  824.3 17.4 %copy-start.20 = (f32[16,128,1]{1,0,2:T(8,128)S(1)}, f32[16,128,1]{1,0,2:T(8,128)}, u32[]{:S(2)}) copy-start(f32[16,128,1]{1,0,2:T(8,128)} %copy-done.19) | copy-start | bytes 24580
  825.6 35.0 %copy-start.23 = (s32[2048,1]{0,1:T(1,128)S(1)}, s32[2048,1]{0,1:T(1,128)}, u32[]{:S(2)}) copy-start(s32[2048,1]{0,1:T(1,128)} %get-tuple-element.167) | copy-start | bytes 24580
  825.6 38.0 %copy-start.39 = (s32[16]{0:T(128)S(1)}, s32[16]{0:T(128)}, u32[]{:S(2)}) copy-start(s32[16]{0:T(128)} %copy-done.38) | copy-start | bytes 196
  825.6 49.2 %copy-start.42 = (s32[16]{0:T(128)S(1)}, s32[16]{0:T(128)}, u32[]{:S(2)}) copy-start(s32[16]{0:T(128)} %param.17) | copy-start | bytes 196
  825.7 61.7 %copy-start.4 = (f32[16,128,128]{1,0,2:T(8,128)S(1)}, f32[16,128,128]{1,0,2:T(8,128)}, u32[]{:S(2)}) copy-start(f32[16,128,128]{1,0,2:T(8,128)} %copy-done.3) | copy-start | bytes 3145732
  835.8 60.2 %all-to-all-start.1 = ((f32[128,128,16]{1,2,0:T(8,128)}), f32[128,128,16]{1,2,0:T(8,128)S(1)}, u32[]{:S(2)}, u32[]{:S(2)}) async-start(f32[128,128,16]{1,2,0:T(8,128)} %multiply_bitcast_fusion.2), calls=%async_computation.1 | async-start | bytes 2097152 | tf_op jit(solution)/shard_map/all_to_all | solution.py:187
  (18 other events, 133.2 us)
where the time goes:
time: 914 us; the launch traced here: 903 us
  blocking collectives  357 us (39%)
  local copies, waits for them, and re-layouts  182 us (20%)
  matrix products  175 us (19%)
  other arithmetic  105 us (11%)
  starting transfers between devices  65.6 us (7%)
  between operations  15.5 us (2%)
    psum x36, blocking collectives, one_axis_at_a_time(): array = lax.psum(array, axis)  321 us
    dot_general x8, matrix products, radiate(): jnp.dot(triangle, thickness.reshape(levels, gpoints * columns), precision...  124 us
    reshape x8, local copies, waits for them, and re-layouts, radiate(): cumulative = cumulative.reshape(levels, gpoints, columns)  67.7 us
    dot_general x8, matrix products, radiate(): jnp.einsum('lgc,g->lc', downward - upward, solar_weight, precision=lax.Pr...  51.3 us
    slice x8, local copies, waits for them, and re-layouts, radiate(): cumulative[-1] - cumulative  49.3 us
    ppermute x14, starting transfers between devices, padded(): after = lax.ppermute(first, axis, down)  28.1 us
    all_gather x3, blocking collectives, stacked_from(): blocks = lax.all_gather(blocks, axes[k])  28 us
    ppermute x14, starting transfers between devices, padded(): before = lax.ppermute(last, axis, up)  25.9 us
  transfers between devices with their start and end apart: 30, of which 6 were waited for; matrix products, arithmetic and copies ran while one was open for 46% of the time, Pallas kernels for 0%

commit v1 on v0

--- a/solution.py
+++ b/solution.py
@@ -25,7 +25,7 @@
 
 def one_axis_at_a_time(array, axes):
     for axis in axes:
-        array = lax.psum(array, axis)
+        array = jnp.sum(lax.all_gather(array, axis), axis=0)
     return array
 
 

time: 914 us -> 961 us (1.051)
  local copies, waits for them, and re-layouts: 182 us -> 239 us
  blocking collectives: 357 us -> 310 us
  other arithmetic: 105 us -> 132 us
    psum x36 -> x0, blocking collectives: 321 us -> none  [one_axis_at_a_time(): array = lax.psum(array, axis)]
    unnamed x1 -> x37, blocking collectives: 7.33 us -> 282 us
    unnamed x96 -> x185, local copies, waits for them, and re-layouts: 8.54 us -> 68.2 us
    reduce_sum x0 -> x40, other arithmetic: none -> 24.4 us  [one_axis_at_a_time(): array = jnp.sum(lax.all_gather(array, axis), axis=0)]
  transfers between devices with their start and end apart: 30 -> 30, of which waited for: 6 -> 6; matrix products, arithmetic and copies ran while one was open for 46% -> 57% of each run, Pallas kernels for 0% -> 0%
where the time goes in v1:
time: 961 us; the launch traced here: 949 us
  blocking collectives  310 us (32%)
  local copies, waits for them, and re-layouts  239 us (25%)
  matrix products  175 us (18%)
  other arithmetic  132 us (14%)
  starting transfers between devices  69.7 us (7%)
  between operations  15.3 us (2%)
    unnamed x37, blocking collectives  282 us
    dot_general x8, matrix products, radiate(): jnp.dot(triangle, thickness.reshape(levels, gpoints * columns), precision...  124 us
    unnamed x185, local copies, waits for them, and re-layouts  68.2 us
    reshape x8, local copies, waits for them, and re-layouts, radiate(): cumulative = cumulative.reshape(levels, gpoints, columns)  67.7 us
    dot_general x8, matrix products, radiate(): jnp.einsum('lgc,g->lc', downward - upward, solar_weight, precision=lax.Pr...  51.3 us
    slice x8, local copies, waits for them, and re-layouts, radiate(): cumulative[-1] - cumulative  49.3 us
    ppermute x14, starting transfers between devices, padded(): before = lax.ppermute(last, axis, up)  28.7 us
    all_gather x3, blocking collectives, stacked_from(): blocks = lax.all_gather(blocks, axes[k])  28 us
  transfers between devices with their start and end apart: 30, of which 6 were waited for; matrix products, arithmetic and copies ran while one was open for 57% of the time, Pallas kernels for 0%

profile of v1, /device:TPU:0, one launch (start us, length us, event | category | flops | bytes accessed | tf_op | source)
XLA Modules:
  0.0 948.8 jit_solution(16375921239434758973)
XLA Ops:
  18.7 7.0 all-reduce.52
  25.8 14.2 %all-gather.4 = s32[4,4,16]{2,1,0:T(4,128)S(1)} all-gather(s32[1,4,16]{2,1,0:T(4,128)S(1)} %reshape.1086), channel_id=3, replica_groups=mesh['gx_0'=4,'gx_1'=2,'gy_0'=4,'gy_1'=4] {'gy_0'}, dimensions={0}, use_global_device_ids=true | all-gather | bytes 1280 | tf_op jit(solution)/shard_map/all_gather | solution.py:41
  40.0 11.9 %all-gather.2 = s32[16,4,16]{2,1,0:T(4,128)S(1)} all-gather(s32[4,4,16]{2,1,0:T(4,128)S(1)} %all-gather.4), channel_id=4, replica_groups=mesh['gx_0'=4,'gx_1'=2,'gy_0'=4,'gy_1'=4] {'gy_1'}, dimensions={0}, use_global_device_ids=true | all-gather | bytes 5120 | tf_op jit(solution)/shard_map/all_gather | solution.py:41
  68.6 8.6 gather_fusion.1
  80.1 7.2 all-to-all-start
  91.9 6.6 gather_fusion
  112.0 6.3 fusion.100
  137.2 10.0 %all-reduce.55 = (f32[4]{0:T(128)S(1)}, f32[4]{0:T(128)S(1)}) all-reduce(f32[4]{0:T(128)S(1)} %dynamic-update-slice.2, f32[4]{0:T(128)S(1)} %dynamic-update-slice.6), channel_id=1, replica_groups=mesh['gx_0'=4,'gx_1'=2,'gy_0'=4,'gy_1'=4] {'gx_0'}, use_global_device_ids=true, to_apply=%add.12 | all-reduce | flops 8 | bytes 64
  160.1 14.4 %all-reduce.54 = (f32[4]{0:T(128)S(1)}, f32[4]{0:T(128)S(1)}) all-reduce(f32[4]{0:T(128)S(1)} %dynamic-update-slice.4, f32[4]{0:T(128)S(1)} %dynamic-update-slice.8), channel_id=1, replica_groups=mesh['gx_0'=4,'gx_1'=2,'gy_0'=4,'gy_1'=4] {'gy_0'}, use_global_device_ids=true, to_apply=%add.14 | all-reduce | flops 8 | bytes 64
  178.5 9.5 %all-reduce.53 = (f32[4]{0:T(128)S(1)}, f32[4]{0:T(128)S(1)}) all-reduce(f32[4]{0:T(128)S(1)} %dynamic-update-slice.5, f32[4]{0:T(128)S(1)} %dynamic-update-slice.9), channel_id=1, replica_groups=mesh['gx_0'=4,'gx_1'=2,'gy_0'=4,'gy_1'=4] {'gy_1'}, use_global_device_ids=true, to_apply=%add.15 | all-reduce | flops 8 | bytes 64
  194.0 7.7 all-reduce.20
  208.1 8.5 all-reduce.22
  218.7 7.7 all-reduce.23
  245.5 9.7 %all-reduce.24 = f32[4]{0:T(128)S(1)} all-reduce(f32[4]{0:T(128)S(1)} %dynamic-update-slice.14), channel_id=1, replica_groups=mesh['gx_0'=4,'gx_1'=2,'gy_0'=4,'gy_1'=4] {'gx_0'}, use_global_device_ids=true, to_apply=%add.24 | all-reduce | flops 4 | bytes 32
  261.5 10.4 %all-reduce.26 = f32[4]{0:T(128)S(1)} all-reduce(f32[4]{0:T(128)S(1)} %dynamic-update-slice.16), channel_id=1, replica_groups=mesh['gx_0'=4,'gx_1'=2,'gy_0'=4,'gy_1'=4] {'gy_0'}, use_global_device_ids=true, to_apply=%add.26 | all-reduce | flops 4 | bytes 32
  273.8 9.2 all-reduce.27
  289.4 7.8 all-reduce.28
  303.4 9.7 %all-reduce.30 = f32[4]{0:T(128)S(1)} all-reduce(f32[4]{0:T(128)S(1)} %dynamic-update-slice.20), channel_id=1, replica_groups=mesh['gx_0'=4,'gx_1'=2,'gy_0'=4,'gy_1'=4] {'gy_0'}, use_global_device_ids=true, to_apply=%add.30 | all-reduce | flops 4 | bytes 32
  315.1 7.7 all-reduce.31
  342.1 9.6 %all-reduce.32 = f32[4]{0:T(128)S(1)} all-reduce(f32[4]{0:T(128)S(1)} %dynamic-update-slice.22), channel_id=1, replica_groups=mesh['gx_0'=4,'gx_1'=2,'gy_0'=4,'gy_1'=4] {'gx_0'}, use_global_device_ids=true, to_apply=%add.32 | all-reduce | flops 4 | bytes 32
  358.2 10.7 %all-reduce.34 = f32[4]{0:T(128)S(1)} all-reduce(f32[4]{0:T(128)S(1)} %dynamic-update-slice.24), channel_id=1, replica_groups=mesh['gx_0'=4,'gx_1'=2,'gy_0'=4,'gy_1'=4] {'gy_0'}, use_global_device_ids=true, to_apply=%add.34 | all-reduce | flops 4 | bytes 32
  370.9 8.3 all-reduce.35
  385.5 8.7 all-reduce.36
  400.6 9.7 %all-reduce.38 = f32[4]{0:T(128)S(1)} all-reduce(f32[4]{0:T(128)S(1)} %dynamic-update-slice.28), channel_id=1, replica_groups=mesh['gx_0'=4,'gx_1'=2,'gy_0'=4,'gy_1'=4] {'gy_0'}, use_global_device_ids=true, to_apply=%add.38 | all-reduce | flops 4 | bytes 32
  412.8 7.7 all-reduce.39
  439.7 8.4 all-reduce.40
  454.4 11.9 %all-reduce.42 = f32[4]{0:T(128)S(1)} all-reduce(f32[4]{0:T(128)S(1)} %dynamic-update-slice.32), channel_id=1, replica_groups=mesh['gx_0'=4,'gx_1'=2,'gy_0'=4,'gy_1'=4] {'gy_0'}, use_global_device_ids=true, to_apply=%add.42 | all-reduce | flops 4 | bytes 32
  468.3 8.0 all-reduce.43
  481.8 9.0 all-reduce.44
  497.8 9.7 %all-reduce.46 = f32[4]{0:T(128)S(1)} all-reduce(f32[4]{0:T(128)S(1)} %dynamic-update-slice.36), channel_id=1, replica_groups=mesh['gx_0'=4,'gx_1'=2,'gy_0'=4,'gy_1'=4] {'gy_0'}, use_global_device_ids=true, to_apply=%add.46 | all-reduce | flops 4 | bytes 32
  510.2 7.7 all-reduce.47
  537.5 325.3 %while.13 = (s32[]{:T(128)}, f32[8,128,128]{2,1,0:T(8,128)}, f32[8,2,128]{2,1,0:T(2,128)S(1)}, f32[128,112]{0,1:T(8,128)S(1)}, f32[8,128,128]{2,1,0:T(8,128)S(1)}, /*index=5*/f32[112]{0:T(128)S(1)}, s32[]{:T(128)}) while((s32[]{:T(128)}, f32[8,128,128]{2,1,0:T(8,128)}, f32[8,2,128]{2,1,0:T(2,128)S(1)}, ...), condition=%wide.region_56.57_spmd.clone, body=%wide.region_55.56_spmd.clone.sunk | while | flops 2860824576 | bytes 88995904 | solution.py:179
  539.9 15.5 %fusion.207 = f32[14336,128]{1,0:T(8,128)} fusion(f32[16,8,112,128]{3,2,1,0:T(8,128)S(1)} %bitcast.158), kind=kOutput, calls=%fused_computation.6.clone.1 | convolution fusion | flops 2818605056 | bytes 14680064 | tf_op jit(solution)/shard_map/while/body/eval_jaxpr/dot_general | solution.py:97
  555.4 8.5 copy.207
  563.9 6.2 slice_reduce_fusion.2
  571.3 6.4 fusion.209
  580.5 15.5 %fusion.207 = f32[14336,128]{1,0:T(8,128)} fusion(f32[16,8,112,128]{3,2,1,0:T(8,128)S(1)} %bitcast.158), kind=kOutput, calls=%fused_computation.6.clone.1 | convolution fusion | flops 2818605056 | bytes 14680064 | tf_op jit(solution)/shard_map/while/body/eval_jaxpr/dot_general | solution.py:97
  596.0 8.5 copy.207
  611.9 6.4 fusion.209
  621.1 15.5 %fusion.207 = f32[14336,128]{1,0:T(8,128)} fusion(f32[16,8,112,128]{3,2,1,0:T(8,128)S(1)} %bitcast.158), kind=kOutput, calls=%fused_computation.6.clone.1 | convolution fusion | flops 2818605056 | bytes 14680064 | tf_op jit(solution)/shard_map/while/body/eval_jaxpr/dot_general | solution.py:97
  636.6 8.5 copy.207
  645.1 6.2 slice_reduce_fusion.2
  652.5 6.4 fusion.209
  661.8 15.5 %fusion.207 = f32[14336,128]{1,0:T(8,128)} fusion(f32[16,8,112,128]{3,2,1,0:T(8,128)S(1)} %bitcast.158), kind=kOutput, calls=%fused_computation.6.clone.1 | convolution fusion | flops 2818605056 | bytes 14680064 | tf_op jit(solution)/shard_map/while/body/eval_jaxpr/dot_general | solution.py:97
  677.3 8.5 copy.207
  693.1 6.4 fusion.209
  702.4 15.5 %fusion.207 = f32[14336,128]{1,0:T(8,128)} fusion(f32[16,8,112,128]{3,2,1,0:T(8,128)S(1)} %bitcast.158), kind=kOutput, calls=%fused_computation.6.clone.1 | convolution fusion | flops 2818605056 | bytes 14680064 | tf_op jit(solution)/shard_map/while/body/eval_jaxpr/dot_general | solution.py:97
  717.9 8.5 copy.207
  726.3 6.2 slice_reduce_fusion.2
  733.8 6.4 fusion.209
  743.0 15.5 %fusion.207 = f32[14336,128]{1,0:T(8,128)} fusion(f32[16,8,112,128]{3,2,1,0:T(8,128)S(1)} %bitcast.158), kind=kOutput, calls=%fused_computation.6.clone.1 | convolution fusion | flops 2818605056 | bytes 14680064 | tf_op jit(solution)/shard_map/while/body/eval_jaxpr/dot_general | solution.py:97
  758.5 8.5 copy.207
  774.4 6.4 fusion.209
  783.6 15.5 %fusion.207 = f32[14336,128]{1,0:T(8,128)} fusion(f32[16,8,112,128]{3,2,1,0:T(8,128)S(1)} %bitcast.158), kind=kOutput, calls=%fused_computation.6.clone.1 | convolution fusion | flops 2818605056 | bytes 14680064 | tf_op jit(solution)/shard_map/while/body/eval_jaxpr/dot_general | solution.py:97
  799.1 8.5 copy.207
  815.0 6.4 fusion.209
  824.2 15.5 %fusion.207 = f32[14336,128]{1,0:T(8,128)} fusion(f32[16,8,112,128]{3,2,1,0:T(8,128)S(1)} %bitcast.158), kind=kOutput, calls=%fused_computation.6.clone.1 | convolution fusion | flops 2818605056 | bytes 14680064 | tf_op jit(solution)/shard_map/while/body/eval_jaxpr/dot_general | solution.py:97
  839.7 8.5 copy.207
  855.6 6.4 fusion.209
  864.2 7.6 gather_fusion.3
  882.5 7.2 multiply_reduce_fusion
  891.0 10.5 %all-reduce.48 = f32[4]{0:T(128)S(1)} all-reduce(f32[4]{0:T(128)S(1)} %dynamic-update-slice.38), channel_id=1, replica_groups=mesh['gx_0'=4,'gx_1'=2,'gy_0'=4,'gy_1'=4] {'gx_0'}, use_global_device_ids=true, to_apply=%add.48 | all-reduce | flops 4 | bytes 32
  908.0 10.4 %all-reduce.50 = f32[4]{0:T(128)S(1)} all-reduce(f32[4]{0:T(128)S(1)} %dynamic-update-slice.40), channel_id=1, replica_groups=mesh['gx_0'=4,'gx_1'=2,'gy_0'=4,'gy_1'=4] {'gy_0'}, use_global_device_ids=true, to_apply=%add.50 | all-reduce | flops 4 | bytes 32
  920.4 10.6 %all-reduce.51 = f32[4]{0:T(128)S(1)} all-reduce(f32[4]{0:T(128)S(1)} %dynamic-update-slice.41), channel_id=1, replica_groups=mesh['gx_0'=4,'gx_1'=2,'gy_0'=4,'gy_1'=4] {'gy_1'}, use_global_device_ids=true, to_apply=%add.51 | all-reduce | flops 4 | bytes 32
  (484 shorter events, 341.0 us)
Async XLA Ops:
  0.6 62.7 %copy-start.45 = (s32[16]{0:T(128)S(1)}, s32[16]{0:T(128)}, u32[]{:S(2)}) copy-start(s32[16]{0:T(128)} %param.17) | copy-start | bytes 196
  0.6 59.6 %copy-start.30 = (f32[16,128]{1,0:T(8,128)S(1)}, f32[16,128]{1,0:T(8,128)}, u32[]{:S(2)}) copy-start(f32[16,128]{1,0:T(8,128)} %param.14) | copy-start | bytes 24580
  0.7 59.6 %copy-start.31 = (f32[16,128]{1,0:T(8,128)S(1)}, f32[16,128]{1,0:T(8,128)}, u32[]{:S(2)}) copy-start(f32[16,128]{1,0:T(8,128)} %param.13) | copy-start | bytes 24580
  1.7 106.1 %collective-permute-start.7 = (f32[1,128,128]{1,0,2:T(1,128)S(1)}, f32[1,128,128]{1,0,2:T(1,128)S(1)}, u32[]{:S(2)}, u32[]{:S(2)}) collective-permute-start(f32[1,128,128]{1,0,2:T(1,128)S(1)} %copy.162), channel_id=1, source_target_pairs={{0,1},{1,2},{2,3},{3,4},{4,5},{5,6},{6,7},{7,8},{8,9},{9,10},{10,1... | collective-permute-start | bytes 196616 | tf_op jit(solution)/shard_map/ppermute | solution.py:20
  5.3 102.5 %collective-permute-start.5 = (f32[1,128,128]{1,0,2:T(1,128)S(1)}, f32[1,128,128]{1,0,2:T(1,128)S(1)}, u32[]{:S(2)}, u32[]{:S(2)}) collective-permute-start(f32[1,128,128]{1,0,2:T(1,128)S(1)} %copy.156), channel_id=1, source_target_pairs={{1,0},{2,1},{3,2},{4,3},{5,4},{6,5},{7,6},{8,7},{9,8},{10,9},{11,1... | collective-permute-start | bytes 196616 | tf_op jit(solution)/shard_map/ppermute | solution.py:21
  9.0 92.1 %collective-permute-start.3 = (f32[16,128,1]{1,0,2:T(8,128)}, f32[16,128,1]{1,0,2:T(8,128)}, u32[]{:S(2)}, u32[]{:S(2)}) collective-permute-start(f32[16,128,1]{1,0,2:T(8,128)} %get-tuple-element.154), channel_id=1, source_target_pairs={{0,16},{16,32},{32,48},{48,64},{64,80},{80,96},{96,112},{112,0},{1... | collective-permute-start | bytes 24584 | tf_op jit(solution)/shard_map/ppermute | solution.py:20
  9.3 91.9 %collective-permute-start.1 = (f32[16,128,1]{1,0,2:T(8,128)}, f32[16,128,1]{1,0,2:T(8,128)}, u32[]{:S(2)}, u32[]{:S(2)}) collective-permute-start(f32[16,128,1]{1,0,2:T(8,128)} %get-tuple-element.153), channel_id=1, source_target_pairs={{16,0},{32,16},{48,32},{64,48},{80,64},{96,80},{112,96},{0,112},{1... | collective-permute-start | bytes 24584 | tf_op jit(solution)/shard_map/ppermute | solution.py:21
  14.3 419.7 %copy-start.1 = (f32[16,128,128]{1,0,2:T(8,128)}, f32[16,128,128]{1,0,2:T(8,128)S(1)}, u32[]{:S(2)}) copy-start(f32[16,128,128]{1,0,2:T(8,128)S(1)} %copy.142) | copy-start | bytes 3145732
  14.9 87.6 %collective-permute-start = (f32[16,128,1]{1,0,2:T(8,128)}, f32[16,128,1]{1,0,2:T(8,128)S(1)}, u32[]{:S(2)}, u32[]{:S(2)}) collective-permute-start(f32[16,128,1]{1,0,2:T(8,128)} %get-tuple-element.152), channel_id=1, source_target_pairs={{16,0},{32,16},{48,32},{64,48},{80,64},{96,80},{112,96},{0,112},{1... | collective-permute-start | bytes 24584 | tf_op jit(solution)/shard_map/ppermute | solution.py:21
  15.9 51.1 %copy-start.37 = (s32[16]{0:T(128)}, s32[16]{0:T(128)S(1)}, u32[]{:S(2)}) copy-start(s32[16]{0:T(128)S(1)} %iota_multiply_fusion) | copy-start | bytes 196
  55.4 21.7 %copy-start.32 = (s32[128]{0:T(128)}, s32[128]{0:T(128)S(1)}, u32[]{:S(2)}) copy-start(s32[128]{0:T(128)S(1)} %get-tuple-element.158) | copy-start | bytes 1540
  80.1 19.1 %copy-start.26 = (s32[2048,1]{0,1:T(1,128)S(1)}, s32[2048,1]{0,1:T(1,128)}, u32[]{:S(2)}) copy-start(s32[2048,1]{0,1:T(1,128)} %get-tuple-element.159) | copy-start | bytes 24580
  80.1 19.7 %copy-start.25 = (s32[2048,1]{0,1:T(1,128)S(1)}, s32[2048,1]{0,1:T(1,128)}, u32[]{:S(2)}) copy-start(s32[2048,1]{0,1:T(1,128)} %get-tuple-element.167) | copy-start | bytes 24580
  80.1 21.1 %copy-start.35 = (f32[16,128,1]{1,0,2:T(8,128)S(1)}, f32[16,128,1]{1,0,2:T(8,128)}, u32[]{:S(2)}) copy-start(f32[16,128,1]{1,0,2:T(8,128)} %get-tuple-element.151) | copy-start | bytes 24580
  80.1 27.0 %copy-start.44 = (s32[16]{0:T(128)S(1)}, s32[16]{0:T(128)}, u32[]{:S(2)}) copy-start(s32[16]{0:T(128)} %copy-done.43) | copy-start | bytes 196
  80.1 450.0 %all-to-all-start = ((f32[128,130,16]{1,2,0:T(8,128)}), f32[128,130,16]{1,2,0:T(8,128)}, u32[]{:S(2)}, u32[]{:S(2)}) async-start(f32[128,130,16]{1,2,0:T(8,128)} %multiply_bitcast_fusion), calls=%async_computation | async-start | bytes 4194304 | tf_op jit(solution)/shard_map/all_to_all | solution.py:166
  90.5 42.7 %copy-start.8 = (f32[16,127,128]{1,0,2:T(8,128)}, f32[16,127,128]{1,0,2:T(8,128)S(1)}, u32[]{:S(2)}) copy-start(f32[16,127,128]{1,0,2:T(8,128)S(1)} %get-tuple-element.126) | copy-start | bytes 3121156
  101.2 6.6 collective-permute-start.2
  101.2 10.8 %collective-permute-start.4 = (f32[1,128,128]{1,0,2:T(1,128)S(1)}, f32[1,128,128]{1,0,2:T(1,128)S(1)}, u32[]{:S(2)}, u32[]{:S(2)}) collective-permute-start(f32[1,128,128]{1,0,2:T(1,128)S(1)} %copy.153), channel_id=1, source_target_pairs={{1,0},{2,1},{3,2},{4,3},{5,4},{6,5},{7,6},{8,7},{9,8},{10,9},{11,1... | collective-permute-start | bytes 196616 | tf_op jit(solution)/shard_map/ppermute | solution.py:21
  102.5 331.5 %copy-start.18 = (f32[16,128,1]{1,0,2:T(8,128)}, f32[16,128,1]{1,0,2:T(8,128)S(1)}, u32[]{:S(2)}) copy-start(f32[16,128,1]{1,0,2:T(8,128)S(1)} %collective-permute-done) | copy-start | bytes 24580
  102.5 9.5 collective-permute-start.6
  107.8 326.2 %copy-start.20 = (f32[16,128,1]{1,0,2:T(8,128)}, f32[16,128,1]{1,0,2:T(8,128)S(1)}, u32[]{:S(2)}) copy-start(f32[16,128,1]{1,0,2:T(8,128)S(1)} %collective-permute-done.2) | copy-start | bytes 24580
  112.0 322.0 %copy-start.13 = (f32[1,128,128]{1,0,2:T(1,128)}, f32[1,128,128]{1,0,2:T(1,128)S(1)}, u32[]{:S(2)}) copy-start(f32[1,128,128]{1,0,2:T(1,128)S(1)} %collective-permute-done.4) | copy-start | bytes 196612
  112.0 322.0 %copy-start.15 = (f32[1,128,128]{1,0,2:T(1,128)}, f32[1,128,128]{1,0,2:T(1,128)S(1)}, u32[]{:S(2)}) copy-start(f32[1,128,128]{1,0,2:T(1,128)S(1)} %collective-permute-done.6) | copy-start | bytes 196612
  118.3 166.5 %copy-start.3 = (f32[16,128,128]{1,0,2:T(8,128)}, f32[16,128,128]{1,0,2:T(8,128)S(1)}, u32[]{:S(2)}) copy-start(f32[16,128,128]{1,0,2:T(8,128)S(1)} %fusion.100) | copy-start | bytes 3145732
  118.5 9.8 %collective-permute-start.11 = (f32[1,128,128]{1,0,2:T(1,128)S(1)}, f32[1,128,128]{1,0,2:T(1,128)S(1)}, u32[]{:S(2)}, u32[]{:S(2)}) collective-permute-start(f32[1,128,128]{1,0,2:T(1,128)S(1)} %get-tuple-element.148), channel_id=1, source_target_pairs={{0,1},{1,2},{2,3},{3,4},{4,5},{5,6},{6,7},{7,8},{8,9},{9,10},{10,1... | collective-permute-start | bytes 196616 | tf_op jit(solution)/shard_map/ppermute | solution.py:20
  122.6 6.2 collective-permute-start.10
  123.9 4.3 collective-permute-start.9
  123.9 4.3 collective-permute-start.8
  229.7 96.3 %copy-start.5 = (f32[16,128,128]{1,0,2:T(8,128)}, f32[16,128,128]{1,0,2:T(8,128)S(1)}, u32[]{:S(2)}) copy-start(f32[16,128,128]{1,0,2:T(8,128)S(1)} %multiply_add_fusion.4) | copy-start | bytes 3145732
  229.8 9.8 %collective-permute-start.15 = (f32[1,128,128]{1,0,2:T(1,128)S(1)}, f32[1,128,128]{1,0,2:T(1,128)S(1)}, u32[]{:S(2)}, u32[]{:S(2)}) collective-permute-start(f32[1,128,128]{1,0,2:T(1,128)S(1)} %get-tuple-element.144), channel_id=1, source_target_pairs={{0,1},{1,2},{2,3},{3,4},{4,5},{5,6},{6,7},{7,8},{8,9},{9,10},{10,1... | collective-permute-start | bytes 196616 | tf_op jit(solution)/shard_map/ppermute | solution.py:20
  233.7 6.2 collective-permute-start.14
  235.0 4.5 collective-permute-start.13
  235.0 4.5 collective-permute-start.12
  326.0 97.8 %copy-start.6 = (f32[16,128,128]{1,0,2:T(8,128)}, f32[16,128,128]{1,0,2:T(8,128)S(1)}, u32[]{:S(2)}) copy-start(f32[16,128,128]{1,0,2:T(8,128)S(1)} %multiply_add_fusion.3) | copy-start | bytes 3145732
  326.1 55.0 %copy-start.12 = (f32[16,128,128]{1,0,2:T(8,128)S(1)}, f32[16,128,128]{1,0,2:T(8,128)}, u32[]{:S(2)}) copy-start(f32[16,128,128]{1,0,2:T(8,128)} %get-tuple-element.121) | copy-start | bytes 3145732
  326.1 9.9 %collective-permute-start.19 = (f32[1,128,128]{1,0,2:T(1,128)S(1)}, f32[1,128,128]{1,0,2:T(1,128)S(1)}, u32[]{:S(2)}, u32[]{:S(2)}) collective-permute-start(f32[1,128,128]{1,0,2:T(1,128)S(1)} %get-tuple-element.140), channel_id=1, source_target_pairs={{0,1},{1,2},{2,3},{3,4},{4,5},{5,6},{6,7},{7,8},{8,9},{9,10},{10,1... | collective-permute-start | bytes 196616 | tf_op jit(solution)/shard_map/ppermute | solution.py:20
  330.2 6.2 collective-permute-start.18
  331.5 4.5 collective-permute-start.17
  331.5 4.5 collective-permute-start.16
  422.4 74.7 %copy-start.24 = (f32[128,16]{0,1:T(8,128)S(1)}, f32[128,16]{0,1:T(8,128)}, u32[]{:S(2)}) copy-start(f32[128,16]{0,1:T(8,128)} %get-tuple-element.162) | copy-start | bytes 24580
  422.4 87.0 %copy-start.34 = (pred[128,16]{0,1:T(8,128)(4,1)S(1)}, pred[128,16]{0,1:T(8,128)(4,1)}, u32[]{:S(2)}) copy-start(pred[128,16]{0,1:T(8,128)(4,1)} %get-tuple-element.161) | copy-start | bytes 6148
  423.8 96.1 %copy-start.7 = (f32[16,128,128]{1,0,2:T(8,128)}, f32[16,128,128]{1,0,2:T(8,128)S(1)}, u32[]{:S(2)}) copy-start(f32[16,128,128]{1,0,2:T(8,128)S(1)} %multiply_add_fusion.2) | copy-start | bytes 3145732
  423.9 9.8 %collective-permute-start.23 = (f32[1,128,128]{1,0,2:T(1,128)S(1)}, f32[1,128,128]{1,0,2:T(1,128)S(1)}, u32[]{:S(2)}, u32[]{:S(2)}) collective-permute-start(f32[1,128,128]{1,0,2:T(1,128)S(1)} %get-tuple-element.136), channel_id=1, source_target_pairs={{0,1},{1,2},{2,3},{3,4},{4,5},{5,6},{6,7},{7,8},{8,9},{9,10},{10,1... | collective-permute-start | bytes 196616 | tf_op jit(solution)/shard_map/ppermute | solution.py:20
  427.9 6.2 collective-permute-start.22
  429.2 4.5 collective-permute-start.21
  429.2 100.9 %copy-start.29 = (s32[1024]{0:T(1024)S(1)}, s32[1024]{0:T(1024)}, u32[]{:S(2)}) copy-start(s32[1024]{0:T(1024)} %broadcast_clamp_fusion.3) | copy-start | bytes 12292
  429.2 4.5 collective-permute-start.20
  438.5 97.9 %copy-start.38 = (pred[8,128]{1,0:T(8,128)(4,1)S(1)}, pred[8,128]{1,0:T(8,128)(4,1)}, u32[]{:S(2)}) copy-start(pred[8,128]{1,0:T(8,128)(4,1)} %compare_and_fusion.3) | copy-start | bytes 3076
  478.1 59.4 %copy-start.17 = (f32[128,112]{0,1:T(8,128)S(1)}, f32[128,112]{0,1:T(8,128)}, u32[]{:S(2)}) copy-start(f32[128,112]{0,1:T(8,128)} %param.15) | copy-start | bytes 172036
  478.1 59.4 %copy-start.47 = (f32[112]{0:T(128)S(1)}, f32[112]{0:T(128)}, u32[]{:S(2)}) copy-start(f32[112]{0:T(128)} %param.16) | copy-start | bytes 1348
  480.5 57.0 %copy-start.11 = (f32[16,128,128]{1,0,2:T(8,128)}, f32[16,128,128]{1,0,2:T(8,128)S(1)}, u32[]{:S(2)}) copy-start(f32[16,128,128]{1,0,2:T(8,128)S(1)} %get-tuple-element.113) | copy-start | bytes 3145732
  520.8 361.7 %collective-permute-start.27 = (f32[1,128,128]{1,0,2:T(1,128)}, f32[1,128,128]{1,0,2:T(1,128)}, u32[]{:S(2)}, u32[]{:S(2)}) collective-permute-start(f32[1,128,128]{1,0,2:T(1,128)} %get-tuple-element.132), channel_id=1, source_target_pairs={{0,1},{1,2},{2,3},{3,4},{4,5},{5,6},{6,7},{7,8},{8,9},{9,10},{10,1... | collective-permute-start | bytes 196616 | tf_op jit(solution)/shard_map/ppermute | solution.py:20
  525.3 357.2 %collective-permute-start.26 = (f32[1,128,128]{1,0,2:T(1,128)}, f32[1,128,128]{1,0,2:T(1,128)}, u32[]{:S(2)}, u32[]{:S(2)}) collective-permute-start(f32[1,128,128]{1,0,2:T(1,128)} %get-tuple-element.131), channel_id=1, source_target_pairs={{1,0},{2,1},{3,2},{4,3},{5,4},{6,5},{7,6},{8,7},{9,8},{10,9},{11,1... | collective-permute-start | bytes 196616 | tf_op jit(solution)/shard_map/ppermute | solution.py:21
  527.2 355.3 %collective-permute-start.25 = (f32[16,128,1]{1,0,2:T(8,128)}, f32[16,128,1]{1,0,2:T(8,128)}, u32[]{:S(2)}, u32[]{:S(2)}) collective-permute-start(f32[16,128,1]{1,0,2:T(8,128)} %get-tuple-element.130), channel_id=1, source_target_pairs={{0,16},{16,32},{32,48},{48,64},{64,80},{80,96},{96,112},{112,0},{1... | collective-permute-start | bytes 24584 | tf_op jit(solution)/shard_map/ppermute | solution.py:20
  527.2 355.3 %collective-permute-start.24 = (f32[16,128,1]{1,0,2:T(8,128)}, f32[16,128,1]{1,0,2:T(8,128)}, u32[]{:S(2)}, u32[]{:S(2)}) collective-permute-start(f32[16,128,1]{1,0,2:T(8,128)} %get-tuple-element.129), channel_id=1, source_target_pairs={{16,0},{32,16},{48,32},{64,48},{80,64},{96,80},{112,96},{0,112},{1... | collective-permute-start | bytes 24584 | tf_op jit(solution)/shard_map/ppermute | solution.py:21
  537.5 326.6 %copy-start.28 = (s32[2048]{0:T(1024)S(1)}, s32[2048]{0:T(1024)}, u32[]{:S(2)}) copy-start(s32[2048]{0:T(1024)} %broadcast_clamp_fusion) | copy-start | bytes 24580
  864.1 18.3 %copy-start.2 = (f32[16,128,128]{1,0,2:T(8,128)S(1)}, f32[16,128,128]{1,0,2:T(8,128)}, u32[]{:S(2)}) copy-start(f32[16,128,128]{1,0,2:T(8,128)} %copy-done.1) | copy-start | bytes 3145732
  864.2 18.3 %copy-start.14 = (f32[1,128,128]{1,0,2:T(1,128)S(1)}, f32[1,128,128]{1,0,2:T(1,128)}, u32[]{:S(2)}) copy-start(f32[1,128,128]{1,0,2:T(1,128)} %copy-done.13) | copy-start | bytes 196612
  864.2 18.3 %copy-start.16 = (f32[1,128,128]{1,0,2:T(1,128)S(1)}, f32[1,128,128]{1,0,2:T(1,128)}, u32[]{:S(2)}) copy-start(f32[1,128,128]{1,0,2:T(1,128)} %copy-done.15) | copy-start | bytes 196612
  864.2 18.3 %copy-start.19 = (f32[16,128,1]{1,0,2:T(8,128)S(1)}, f32[16,128,1]{1,0,2:T(8,128)}, u32[]{:S(2)}) copy-start(f32[16,128,1]{1,0,2:T(8,128)} %copy-done.18) | copy-start | bytes 24580
  871.8 48.6 %copy-start.46 = (s32[16]{0:T(128)S(1)}, s32[16]{0:T(128)}, u32[]{:S(2)}) copy-start(s32[16]{0:T(128)} %param.17) | copy-start | bytes 196
  871.8 61.1 %copy-start.4 = (f32[16,128,128]{1,0,2:T(8,128)S(1)}, f32[16,128,128]{1,0,2:T(8,128)}, u32[]{:S(2)}) copy-start(f32[16,128,128]{1,0,2:T(8,128)} %copy-done.3) | copy-start | bytes 3145732
  874.4 67.0 %all-to-all-start.1 = ((f32[128,128,16]{1,2,0:T(8,128)}), f32[128,128,16]{1,2,0:T(8,128)S(1)}, u32[]{:S(2)}, u32[]{:S(2)}) async-start(f32[128,128,16]{1,2,0:T(8,128)} %multiply_bitcast_fusion.2), calls=%async_computation.1 | async-start | bytes 2097152 | tf_op jit(solution)/shard_map/all_to_all | solution.py:187
  (21 other events, 162.9 us)
